TPU v7x, 128 devices: a whole 4x4x4 slice. The times are simulated.
128 devices in a mesh: pipe: 4 (over y), dp: 32 (over x, z, core).
Axes of the slice: x: 4, y: 4, z: 4, core: 2. Of those that a mesh axis runs over, the one named last changes fastest.
Arguments:
- queries: bfloat16 [4, 2, 16384, 4096], P('pipe', None, 'dp'), may hold values from -64 to 64
- keys: bfloat16 [4, 2, 16384, 512], P('pipe', None, 'dp'), may hold values from -6 to 6
- values: bfloat16 [4, 2, 16384, 512], P('pipe', None, 'dp'), may hold values from -6 to 6
- segment: int32 [4, 2, 16384], P('pipe', None, 'dp'), may hold values from 0 to 16383, as said below
- parent: int32 [4, 2, 16384], P('pipe', None, 'dp'), may hold values from 0 to 16382, as said below
- tree_lengths: int32 [4, 2, 128], P('pipe'), may hold values from 0 to 3, as said below
Outputs:
- forward_next: bfloat16 [4, 16384, 4096], P('pipe', 'dp')
- return_next: bfloat16 [4, 16384, 4096], P('pipe', 'dp')
Inputs may be any that keep to these rules, and one draw needn't show every extreme that they name: `tree_lengths`: each row lists the trees of one micro-batch in order: entries of 1 to 3 blocks that sum to 128, then zeros; some tree is exactly 3 blocks long. Within a micro-batch a segment is a run of rows, numbered by the index of its first row; every tree's first row opens a new segment, so no segment spans two trees; the last row of every micro-batch opens a segment of its own. The first segment of a tree is its own parent; every other segment's parent is an earlier segment of the same tree whose parent is that first segment; in every micro-batch the last row's parent is the segment opened by the row before it.
All inputs are finite; a program needn't handle non-finite values.
Results may differ from a plain program's by a relative error of at most 0.0036.
Values may be sent and summed in bfloat16 or wider, within the bound.
A program may use at most 192 MiB of HBM per device.

v0:
```python
import math

import jax
import jax.numpy as jnp
from jax import lax
from jax.sharding import PartitionSpec as P

BLK = 128
TREE_MOST = 3
KV_HEADS = 4
GROUP = 8
HEAD = 128


NEG = -1e30


def shifted(value, axis, steps):
    count = lax.axis_size(axis)
    initial, last = (max(0, -steps), min(count, count - steps))
    return lax.ppermute(value, axis, [(source, source + steps) for source in range(initial, last)])


def block_trees(lengths, block_ids):
    ends = jnp.cumsum(lengths)
    starts = ends - lengths
    inside = (starts[None, :] <= block_ids[:, None]) & (lengths[None, :] > 0)
    tree = jnp.sum(inside.astype(jnp.int32), axis=1) - 1
    begins = jnp.max(jnp.where(inside, starts[None, :], -1), axis=1)
    present = (block_ids >= 0) & (block_ids < lengths.shape[0])
    return (jnp.where(present, tree, -1), begins)


def pad_front(array, fill, reach):
    padding = jnp.full((reach,) + array.shape[1:], fill, array.dtype)
    return jnp.concatenate([padding, array], axis=0)


def attend(queries, query_info, keys, values, key_info, offset):
    reach = (TREE_MOST - 1) * BLK
    span = TREE_MOST * BLK
    count = queries.shape[0] // BLK
    key_rows = pad_front(keys, 0, reach)
    value_rows = pad_front(values, 0, reach)
    key_tree = pad_front(key_info[0], -2, reach)
    key_pos = pad_front(key_info[1], -1, reach)
    key_seg = pad_front(key_info[2], -3, reach)
    key_par = pad_front(key_info[3], -4, reach)
    scale = 1.0 / math.sqrt(HEAD)
    pieces = []
    for group_start in range(0, count, 4):
        group_count = min(4, count - group_start)
        chosen = range(group_start, group_start + group_count)

        def windowed(rows):
            return jnp.stack(
                [
                    lax.slice_in_dim(
                        rows, (index + offset) * BLK, (index + offset) * BLK + span, axis=0
                    )
                    for index in chosen
                ]
            )

        keyset = windowed(key_rows).reshape(group_count, span, KV_HEADS, HEAD)
        valueset = windowed(value_rows).reshape(group_count, span, KV_HEADS, HEAD)
        window_tree = windowed(key_tree)
        window_pos = windowed(key_pos)
        window_seg = windowed(key_seg)
        window_par = windowed(key_par)
        first_row = group_start * BLK
        last_row = first_row + group_count * BLK
        query = queries[first_row:last_row].reshape(group_count, BLK, KV_HEADS, GROUP, HEAD)
        query_tree = query_info[0][first_row:last_row].reshape(group_count, BLK)
        query_pos = query_info[1][first_row:last_row].reshape(group_count, BLK)
        query_seg = query_info[2][first_row:last_row].reshape(group_count, BLK)
        query_par = query_info[3][first_row:last_row].reshape(group_count, BLK)
        related = (
            (window_seg[:, None, :] == query_seg[:, :, None])
            | (window_seg[:, None, :] == query_par[:, :, None])
            | (window_par == window_seg)[:, None, :]
        )
        allowed = (
            (window_tree[:, None, :] == query_tree[:, :, None])
            & (window_pos[:, None, :] <= query_pos[:, :, None])
            & related
        )
        scores = (
            jnp.einsum("aqhgd,akhd->ahgqk", query, keyset, preferred_element_type=jnp.float32)
            * scale
        )
        scores = jnp.where(allowed[:, None, None], scores, NEG)
        top = jnp.max(scores, axis=-1, keepdims=True)
        weights = jnp.exp(scores - top)
        totals = jnp.sum(weights, axis=-1)
        rounded = weights.astype(jnp.bfloat16)
        mixed = jnp.einsum(
            "ahgqk,akhd->aqhgd", rounded, valueset, preferred_element_type=jnp.float32
        )
        totals = jnp.transpose(totals, (0, 3, 1, 2))[..., None]
        pieces.append((mixed / totals).astype(jnp.bfloat16).reshape(group_count * BLK, -1))
    return jnp.concatenate(pieces, axis=0)


def section(queries, keys, values, segment, parent, lengths):
    rows = queries.shape[0]
    span_blocks = rows // BLK
    reach_blocks = TREE_MOST - 1
    reach = reach_blocks * BLK
    first_block = lax.axis_index("dp") * span_blocks
    moved = shifted(
        (queries[:reach], keys[:reach], values[:reach], segment[:reach], parent[:reach]), "dp", -1
    )
    all_queries = jnp.concatenate([queries, moved[0]], axis=0)
    all_keys = jnp.concatenate([keys, moved[1]], axis=0)
    all_values = jnp.concatenate([values, moved[2]], axis=0)
    all_seg = jnp.concatenate([segment, moved[3]], axis=0)
    all_par = jnp.concatenate([parent, moved[4]], axis=0)
    block_ids = first_block + jnp.arange(span_blocks + reach_blocks, dtype=jnp.int32)
    tree, begins = block_trees(lengths, block_ids)
    positions = first_block * BLK + jnp.arange(rows + reach, dtype=jnp.int32)
    info = (jnp.repeat(tree, BLK), positions, all_seg, all_par)
    result = attend(all_queries, info, all_keys, all_values, info, 0)
    returned = shifted(result[rows:], "dp", 1)
    own_start = jnp.repeat(begins[:span_blocks], BLK) >= first_block
    filled = jnp.concatenate(
        [returned, jnp.zeros((rows - reach, returned.shape[1]), jnp.bfloat16)], axis=0
    )
    return jnp.where(own_start[:, None], result[:rows], filled)


def on_device(queries, keys, values, segment, parent, tree_lengths):
    outgoing = section(
        queries[0, 0], keys[0, 0], values[0, 0], segment[0, 0], parent[0, 0], tree_lengths[0, 0]
    )
    moved_on = shifted(outgoing, "pipe", 1)
    returning = section(
        queries[0, 1], keys[0, 1], values[0, 1], segment[0, 1], parent[0, 1], tree_lengths[0, 1]
    )
    moved_back = shifted(returning, "pipe", -1)
    place = lax.axis_index("pipe")
    forward_next = jnp.where(place == 0, returning, moved_on)
    return_next = jnp.where(place == lax.axis_size("pipe") - 1, outgoing, moved_back)
    return (forward_next[None], return_next[None])


def solution(mesh):
    return jax.shard_map(
        on_device,
        mesh=mesh,
        in_specs=(
            P("pipe", None, "dp", None),
            P("pipe", None, "dp", None),
            P("pipe", None, "dp", None),
            P("pipe", None, "dp"),
            P("pipe", None, "dp"),
            P("pipe", None, None),
        ),
        out_specs=(P("pipe", "dp", None), P("pipe", "dp", None)),
        check_vma=False,
    )
```

profile of v0, /device:TPU:54, one launch (start us, length us, event | category | flops | bytes accessed | tf_op | source)
XLA Modules:
  0.0 487.6 jit_solution(921028909488569772)
XLA Ops:
  5.4 2.1 collective-permute-start.2
  7.5 5.7 %collective-permute-start.7 = (s32[256]{0:T(256)}, s32[256]{0:T(256)}, u32[]{:S(2)}, u32[]{:S(2)}) collective-permute-start(s32[256]{0:T(256)} %bitcast.83), channel_id=1, source_target_pairs={{1,0},{2,1},{3,2},{4,3},{5,4},{6,5},{7,6},{8,7},{9,8},{10,9},{11,1... | collective-permute-start | bytes 3080 | tf_op jit(solution)/shard_map/ppermute | solution.py:21
  13.1 2.6 collective-permute-start.8
  28.3 2.4 fusion.114
  36.5 2.5 slice_bitcast_fusion.2
  38.9 3.9 slice_bitcast_fusion
  64.4 5.7 %copy.146 = bf16[64,8,32,128]{3,2,1,0:T(8,128)(2,1)} copy(bf16[64,8,32,128]{3,1,2,0:T(8,128)(2,1)} %get-tuple-element.12) | data formatting | bytes 8388608
  82.3 3.3 fusion.89
  87.9 5.5 %copy.140 = bf16[64,8,32,128]{3,2,1,0:T(8,128)(2,1)} copy(bf16[64,8,32,128]{3,1,2,0:T(8,128)(2,1)} %get-tuple-element.13) | data formatting | bytes 8388608
  95.3 2.4 collective-permute-start.10
  101.0 2.1 collective-permute-start.6
  106.5 2.2 fusion.95
  108.7 21.1 %collective-permute-done.3 = bf16[256,512]{0,1:T(8,128)(2,1)S(1)} collective-permute-done((bf16[256,512]{0,1:T(8,128)(2,1)S(1)}, bf16[256,512]{0,1:T(8,128)(2,1)S(1)}, u32[]{:S(2)}, u32[]{:S(2)}) %collective-permute-start.3) | collective-permute-done | bytes 262176 | tf_op jit(solution)/shard_map/ppermute | solution.py:21
  129.9 4.0 collective-permute-start.4
  133.8 2.2 fusion.92
  139.9 2.9 fusion.91
  144.7 1.9 copy.74
  146.6 14.6 %fusion.4 = (f32[4,4,8,128]{3,2,1,0:T(8,128)S(1)}, f32[4,4,384,128,8]{3,2,4,1,0:T(8,128)}) fusion(pred[4,128,384]{1,2,0:T(8,128)(4,1)} %get-tuple-element.47, bf16[4,128,4,8,128]{4,3,2,1,0:T(8,128)(2,1)} %bitcast.287, bf16[1,384,4,128]{3,1,2,0:T(8,128)(2,1)} %copy.83, bf16[1,384,4,128]{3,1,2,0:T(8,128)(2,1)} %copy.82, bf16[1,384,4,128]{3,1,2,0:T(8,128)(2,1)} %copy.81, ...), kind=kOutput, calls=%fused_computation.8 | convolution fusion | flops 1635762176 | bytes 31195136 | tf_op jit(solution)/shard_map/aqhgd,akhd->ahgqk/dot_general | solution.py:89
  161.2 11.5 %fusion = f32[4,4,8,128]{3,2,1,0:T(8,128)S(1)} fusion(f32[4,4,384,128,8]{3,2,4,1,0:T(8,128)} %get-tuple-element.107, f32[4,4,8,128]{3,2,1,0:T(8,128)S(1)} %get-tuple-element.106, pred[4,128,384]{1,2,0:T(8,128)(4,1)S(1)} %copy-done.14), kind=kLoop, calls=%fused_computation.4 | loop fusion | flops 25149440 | bytes 25493504 | tf_op jit(solution)/shard_map/reduce_sum | solution.py:95
  172.8 13.4 %fusion.25 = bf16[4,128,4,8,128]{1,4,3,2,0:T(8,128)(2,1)} fusion(f32[4,128,4,8]{1,3,2,0:T(8,128)S(1)} %bitcast.319, f32[4,4,384,128,8]{3,2,4,1,0:T(8,128)} %get-tuple-element.107, f32[4,4,8,128]{3,2,1,0:T(8,128)S(1)} %get-tuple-element.106, pred[4,128,384]{1,2,0:T(8,128)(4,1)S(1)} %copy-done.14, bf16[1,384,4,128]{1,3,2,0:T(8,128)(2,1)S(1)} %bitcast.308, ...), kind=kOutput, calls=%fused_computation.33 | convolution fusion | flops 1646264320 | bytes 31260672 | tf_op jit(solution)/shard_map/ahgqk,akhd->aqhgd/dot_general | solution.py:97
  186.2 2.3 fusion.90
  188.5 2.0 copy.113
  208.0 7.8 %copy.86 = bf16[4,128,4,8,128]{4,3,2,1,0:T(8,128)(2,1)} copy(bf16[4,128,4,8,128]{1,4,3,2,0:T(8,128)(2,1)} %fusion.25) | data formatting | bytes 8388608 | tf_op jit(solution)/shard_map/convert_element_type | solution.py:101
  215.8 7.4 %reshape.519 = bf16[512,4096]{1,0:T(8,128)(2,1)} reshape(bf16[4,128,4,8,128]{4,3,2,1,0:T(8,128)(2,1)} %copy.86) | data formatting | bytes 8388608 | tf_op jit(solution)/shard_map/reshape | solution.py:101
  223.2 14.6 %fusion.5 = (f32[4,4,8,128]{3,2,1,0:T(8,128)S(1)}, f32[4,4,384,128,8]{3,2,4,1,0:T(8,128)}) fusion(pred[4,128,384]{1,2,0:T(8,128)(4,1)S(1)} %copy-done.13, bf16[4,128,4,8,128]{4,3,2,1,0:T(8,128)(2,1)} %bitcast.286, bf16[1,384,4,128]{3,1,2,0:T(8,128)(2,1)S(1)} %copy-done.20, bf16[1,384,4,128]{3,1,2,0:T(8,128)(2,1)S(1)} %copy-done.19, ...), kind=kOutput, calls=%fused_computation.9 | convolution fusion | flops 1635762176 | bytes 31195136 | tf_op jit(solution)/shard_map/aqhgd,akhd->ahgqk/dot_general | solution.py:89
  238.9 2.8 fusion.22
  241.7 3.4 fusion.18
  245.1 4.6 fusion.39
  249.7 3.4 copy.94
  253.2 2.3 reshape.521
  257.4 12.5 %fusion.2 = f32[4,4,8,128]{3,2,1,0:T(8,128)} fusion(f32[4,4,384,128,8]{3,2,4,1,0:T(8,128)} %get-tuple-element.111, f32[4,4,8,128]{3,2,1,0:T(8,128)S(1)} %get-tuple-element.110, pred[4,128,384]{1,2,0:T(8,128)(4,1)S(1)} %copy-done.13), kind=kLoop, calls=%fused_computation.6 | loop fusion | flops 25149440 | bytes 25493504 | tf_op jit(solution)/shard_map/reduce_sum | solution.py:95
  269.9 2.1 copy.149
  272.1 2.7 fusion.23
  274.8 8.2 %collective-permute-done.5 = bf16[256,4096]{1,0:T(8,128)(2,1)S(1)} collective-permute-done((bf16[256,4096]{1,0:T(8,128)(2,1)}, bf16[256,4096]{1,0:T(8,128)(2,1)S(1)}, u32[]{:S(2)}, u32[]{:S(2)}) %collective-permute-start.5) | collective-permute-done | bytes 2097184 | tf_op jit(solution)/shard_map/ppermute | solution.py:21
  283.0 4.1 pad_select_fusion.1
  287.1 2.3 collective-permute-start.13
  289.5 3.5 fusion.20
  293.1 4.6 fusion.38
  297.7 3.5 copy.117
  301.2 2.3 reshape.528
  303.5 2.1 collective-permute-start.11
  305.7 13.1 %fusion.24 = bf16[4,128,4,8,128]{1,4,3,2,0:T(8,128)(2,1)} fusion(f32[4,128,4,8]{1,3,2,0:T(8,128)} %bitcast.318, f32[4,4,384,128,8]{3,2,4,1,0:T(8,128)} %get-tuple-element.111, f32[4,4,8,128]{3,2,1,0:T(8,128)S(1)} %get-tuple-element.110, pred[4,128,384]{1,2,0:T(8,128)(4,1)S(1)} %copy-done.13, bf16[1,384,4,128]{1,3,2,0:T(8,128)(2,1)S(1)} %bitcast.306, ...), kind=kOutput, calls=%fused_computation.31 | convolution fusion | flops 1646264320 | bytes 31260672 | tf_op jit(solution)/shard_map/ahgqk,akhd->aqhgd/dot_general | solution.py:97
  318.8 7.9 %copy.109 = bf16[4,128,4,8,128]{4,3,2,1,0:T(8,128)(2,1)} copy(bf16[4,128,4,8,128]{1,4,3,2,0:T(8,128)(2,1)} %fusion.24) | data formatting | bytes 8388608 | tf_op jit(solution)/shard_map/convert_element_type | solution.py:101
  326.7 7.3 %reshape.526 = bf16[512,4096]{1,0:T(8,128)(2,1)} reshape(bf16[4,128,4,8,128]{4,3,2,1,0:T(8,128)(2,1)} %copy.109) | data formatting | bytes 8388608 | tf_op jit(solution)/shard_map/reshape | solution.py:101
  333.9 47.2 %collective-permute-done.13 = bf16[512,4096]{1,0:T(8,128)(2,1)} collective-permute-done((bf16[512,4096]{1,0:T(8,128)(2,1)}, bf16[512,4096]{1,0:T(8,128)(2,1)}, u32[]{:S(2)}, u32[]{:S(2)}) %collective-permute-start.13) | collective-permute-done | bytes 4194336 | tf_op jit(solution)/shard_map/ppermute | solution.py:21
  381.2 8.4 %select_bitcast_fusion = (bf16[1,512,4096]{2,1,0:T(8,128)(2,1)}, bf16[512,4096]{1,0:T(8,128)(2,1)}) fusion(bf16[512,4096]{1,0:T(8,128)(2,1)} %collective-permute-done.13, pred[]{:T(512)S(6)} %eq.291, bf16[512,4096]{1,0:T(8,128)(2,1)} %reshape.526, bf16[256,4096]{1,0:T(8,128)(2,1)S(1)} %collective-permute-done.11, pred[512]{0:T(512)(128)(4,1)S(1)} %copy-done.48), kind=kLoop, calls=%fused_computation.52 | loop fusion | flops 4194304 | bytes 18874880 | tf_op jit(solution)/shard_map/broadcast_in_dim | solution.py:144
  391.5 91.3 %collective-permute-done.12 = bf16[512,4096]{1,0:T(8,128)(2,1)} collective-permute-done((bf16[512,4096]{1,0:T(8,128)(2,1)}, bf16[512,4096]{1,0:T(8,128)(2,1)}, u32[]{:S(2)}, u32[]{:S(2)}) %collective-permute-start.12) | collective-permute-done | bytes 4194336 | tf_op jit(solution)/shard_map/ppermute | solution.py:21
  482.7 4.6 select_bitcast_fusion.1
  (257 shorter events, 95.6 us)
Async XLA Ops:
  0.6 32.4 %copy-start.33 = (s32[1,2,512]{2,1,0:T(2,128)S(1)}, s32[1,2,512]{2,1,0:T(2,128)}, u32[]{:S(2)}) copy-start(s32[1,2,512]{2,1,0:T(2,128)} %param.9) | copy-start | bytes 12292
  0.6 33.0 %copy-start.34 = (s32[1,2,512]{2,1,0:T(2,128)S(1)}, s32[1,2,512]{2,1,0:T(2,128)}, u32[]{:S(2)}) copy-start(s32[1,2,512]{2,1,0:T(2,128)} %param.10) | copy-start | bytes 12292
  0.7 34.8 %copy-start.2 = (bf16[1,2,512,512]{3,2,1,0:T(8,128)(2,1)S(1)}, bf16[1,2,512,512]{3,2,1,0:T(8,128)(2,1)}, u32[]{:S(2)}) copy-start(bf16[1,2,512,512]{3,2,1,0:T(8,128)(2,1)} %param.7) | copy-start | bytes 3145732
  0.7 30.1 %copy-start.3 = (bf16[1,2,512,512]{3,2,1,0:T(8,128)(2,1)S(1)}, bf16[1,2,512,512]{3,2,1,0:T(8,128)(2,1)}, u32[]{:S(2)}) copy-start(bf16[1,2,512,512]{3,2,1,0:T(8,128)(2,1)} %param.8) | copy-start | bytes 3145732
  2.1 93.2 %collective-permute-start.1 = (s32[256]{0:T(256)}, s32[256]{0:T(256)}, u32[]{:S(2)}, u32[]{:S(2)}) collective-permute-start(s32[256]{0:T(256)} %bitcast.36), channel_id=1, source_target_pairs={{1,0},{2,1},{3,2},{4,3},{5,4},{6,5},{7,6},{8,7},{9,8},{10,9},{11,1... | collective-permute-start | bytes 3080 | tf_op jit(solution)/shard_map/ppermute | solution.py:21
  5.4 93.0 %collective-permute-start.2 = (s32[256]{0:T(256)}, s32[256]{0:T(256)}, u32[]{:S(2)}, u32[]{:S(2)}) collective-permute-start(s32[256]{0:T(256)} %bitcast.38), channel_id=1, source_target_pairs={{1,0},{2,1},{3,2},{4,3},{5,4},{6,5},{7,6},{8,7},{9,8},{10,9},{11,1... | collective-permute-start | bytes 3080 | tf_op jit(solution)/shard_map/ppermute | solution.py:21
  7.5 93.5 %collective-permute-start.7 = (s32[256]{0:T(256)}, s32[256]{0:T(256)}, u32[]{:S(2)}, u32[]{:S(2)}) collective-permute-start(s32[256]{0:T(256)} %bitcast.83), channel_id=1, source_target_pairs={{1,0},{2,1},{3,2},{4,3},{5,4},{6,5},{7,6},{8,7},{9,8},{10,9},{11,1... | collective-permute-start | bytes 3080 | tf_op jit(solution)/shard_map/ppermute | solution.py:21
  13.1 90.7 %collective-permute-start.8 = (s32[256]{0:T(256)}, s32[256]{0:T(256)}, u32[]{:S(2)}, u32[]{:S(2)}) collective-permute-start(s32[256]{0:T(256)} %bitcast.85), channel_id=1, source_target_pairs={{1,0},{2,1},{3,2},{4,3},{5,4},{6,5},{7,6},{8,7},{9,8},{10,9},{11,1... | collective-permute-start | bytes 3080 | tf_op jit(solution)/shard_map/ppermute | solution.py:21
  18.4 167.9 %collective-permute-start.9 = (bf16[256,512]{0,1:T(8,128)(2,1)}, bf16[256,512]{0,1:T(8,128)(2,1)}, u32[]{:S(2)}, u32[]{:S(2)}) collective-permute-start(bf16[256,512]{0,1:T(8,128)(2,1)} %bitcast.87), channel_id=1, source_target_pairs={{1,0},{2,1},{3,2},{4,3},{5,4},{6,5},{7,6},{8,7},{9,8},{10,9},{11,1... | collective-permute-start | bytes 786440 | tf_op jit(solution)/shard_map/ppermute | solution.py:21
  24.1 10.7 %copy-start.35 = (s32[6]{0:T(128)}, s32[6]{0:T(128)S(1)}, u32[]{:S(2)}) copy-start(s32[6]{0:T(128)S(1)} %get-tuple-element.118) | copy-start | bytes 76
  24.1 10.7 %copy-start.36 = (s32[6]{0:T(128)}, s32[6]{0:T(128)S(1)}, u32[]{:S(2)}) copy-start(s32[6]{0:T(128)S(1)} %get-tuple-element.119) | copy-start | bytes 76
  28.3 8.1 %copy-start = (bf16[1,2,512,4096]{3,2,1,0:T(8,128)(2,1)S(1)}, bf16[1,2,512,4096]{3,2,1,0:T(8,128)(2,1)}, u32[]{:S(2)}) copy-start(bf16[1,2,512,4096]{3,2,1,0:T(8,128)(2,1)} %param.6) | copy-start | bytes 25165828
  38.9 8.7 %copy-start.6 = (bf16[1,1,512,512]{3,2,1,0:T(8,128)(2,1)S(1)}, bf16[1,1,512,512]{3,2,1,0:T(8,128)(2,1)}, u32[]{:S(2)}) copy-start(bf16[1,1,512,512]{3,2,1,0:T(8,128)(2,1)} %get-tuple-element.24) | copy-start | bytes 1572868
  42.8 7.0 %copy-start.38 = (s32[768]{0:T(1024)S(1)}, s32[768]{0:T(1024)}, u32[]{:S(2)}) copy-start(s32[768]{0:T(1024)} %broadcast_bitcast_fusion.1) | copy-start | bytes 9220
  42.8 8.1 %copy-start.41 = (s32[3]{0:T(128)S(1)}, s32[3]{0:T(128)}, u32[]{:S(2)}) copy-start(s32[3]{0:T(128)} %get-tuple-element.100) | copy-start | bytes 40
  42.8 8.8 %copy-start.40 = (s32[3]{0:T(128)S(1)}, s32[3]{0:T(128)}, u32[]{:S(2)}) copy-start(s32[3]{0:T(128)} %get-tuple-element.101) | copy-start | bytes 40
  42.8 9.4 %copy-start.37 = (s32[768]{0:T(1024)S(1)}, s32[768]{0:T(1024)}, u32[]{:S(2)}) copy-start(s32[768]{0:T(1024)} %broadcast_bitcast_fusion) | copy-start | bytes 9220
  64.4 7.5 %copy-start.5 = (bf16[1,1,512,512]{3,2,1,0:T(8,128)(2,1)S(1)}, bf16[1,1,512,512]{3,2,1,0:T(8,128)(2,1)}, u32[]{:S(2)}) copy-start(bf16[1,1,512,512]{3,2,1,0:T(8,128)(2,1)} %get-tuple-element.25) | copy-start | bytes 1572868
  64.4 21.2 %copy-start.8 = (bf16[1,1,384,512]{3,2,1,0:T(8,128)(2,1)S(1)}, bf16[1,1,384,512]{3,2,1,0:T(8,128)(2,1)}, u32[]{:S(2)}) copy-start(bf16[1,1,384,512]{3,2,1,0:T(8,128)(2,1)} %get-tuple-element.29) | copy-start | bytes 1179652
  87.9 18.6 %copy-start.39 = (s32[2,128]{1,0:T(2,128)S(1)}, s32[2,128]{1,0:T(2,128)}, u32[]{:S(2)}) copy-start(s32[2,128]{1,0:T(2,128)} %slice_bitcast_fusion.17) | copy-start | bytes 3076
  87.9 18.6 %copy-start.49 = (s32[2]{0:T(128)S(1)}, s32[2]{0:T(128)}, u32[]{:S(2)}) copy-start(s32[2]{0:T(128)} %slice.449) | copy-start | bytes 28
  87.9 18.6 %copy-start.50 = (s32[2]{0:T(128)S(1)}, s32[2]{0:T(128)}, u32[]{:S(2)}) copy-start(s32[2]{0:T(128)} %slice.501) | copy-start | bytes 28
  95.3 174.6 %collective-permute-start.10 = (bf16[256,4096]{1,0:T(8,128)(2,1)}, bf16[256,4096]{1,0:T(8,128)(2,1)}, u32[]{:S(2)}, u32[]{:S(2)}) collective-permute-start(bf16[256,4096]{1,0:T(8,128)(2,1)} %get-tuple-element.10), channel_id=1, source_target_pairs={{1,0},{2,1},{3,2},{4,3},{5,4},{6,5},{7,6},{8,7},{9,8},{10,9},{11,1... | collective-permute-start | bytes 6291464 | tf_op jit(solution)/shard_map/ppermute | solution.py:21
  98.3 41.5 %collective-permute-start = (bf16[256,512]{1,0:T(8,128)(2,1)}, bf16[256,512]{1,0:T(8,128)(2,1)}, u32[]{:S(2)}, u32[]{:S(2)}) collective-permute-start(bf16[256,512]{1,0:T(8,128)(2,1)} %get-tuple-element.15), channel_id=1, source_target_pairs={{1,0},{2,1},{3,2},{4,3},{5,4},{6,5},{7,6},{8,7},{9,8},{10,9},{11,1... | collective-permute-start | bytes 786440 | tf_op jit(solution)/shard_map/ppermute | solution.py:21
  101.0 38.9 %collective-permute-start.6 = (bf16[256,512]{1,0:T(8,128)(2,1)}, bf16[256,512]{1,0:T(8,128)(2,1)}, u32[]{:S(2)}, u32[]{:S(2)}) collective-permute-start(bf16[256,512]{1,0:T(8,128)(2,1)} %get-tuple-element.14), channel_id=1, source_target_pairs={{1,0},{2,1},{3,2},{4,3},{5,4},{6,5},{7,6},{8,7},{9,8},{10,9},{11,1... | collective-permute-start | bytes 786440 | tf_op jit(solution)/shard_map/ppermute | solution.py:21
  103.8 26.1 %collective-permute-start.3 = (bf16[256,512]{0,1:T(8,128)(2,1)S(1)}, bf16[256,512]{0,1:T(8,128)(2,1)S(1)}, u32[]{:S(2)}, u32[]{:S(2)}) collective-permute-start(bf16[256,512]{0,1:T(8,128)(2,1)S(1)} %bitcast.317), channel_id=1, source_target_pairs={{1,0},{2,1},{3,2},{4,3},{5,4},{6,5},{7,6},{8,7},{9,8},{10,9},{11,1... | collective-permute-start | bytes 786440 | tf_op jit(solution)/shard_map/ppermute | solution.py:21
  129.9 107.9 %collective-permute-start.4 = (bf16[256,4096]{1,0:T(8,128)(2,1)}, bf16[256,4096]{1,0:T(8,128)(2,1)S(1)}, u32[]{:S(2)}, u32[]{:S(2)}) collective-permute-start(bf16[256,4096]{1,0:T(8,128)(2,1)} %get-tuple-element.11), channel_id=1, source_target_pairs={{1,0},{2,1},{3,2},{4,3},{5,4},{6,5},{7,6},{8,7},{9,8},{10,9},{11,1... | collective-permute-start | bytes 6291464 | tf_op jit(solution)/shard_map/ppermute | solution.py:21
  146.6 14.6 %copy-start.14 = (pred[4,128,384]{1,2,0:T(8,128)(4,1)S(1)}, pred[4,128,384]{1,2,0:T(8,128)(4,1)}, u32[]{:S(2)}) copy-start(pred[4,128,384]{1,2,0:T(8,128)(4,1)} %get-tuple-element.47) | copy-start | bytes 589828
  161.2 11.6 %copy-start.21 = (bf16[1,1,384,512]{2,3,1,0:T(8,128)(2,1)S(1)}, bf16[1,1,384,512]{2,3,1,0:T(8,128)(2,1)}, u32[]{:S(2)}) copy-start(bf16[1,1,384,512]{2,3,1,0:T(8,128)(2,1)} %copy.75) | copy-start | bytes 1179652
  161.2 11.6 %copy-start.22 = (bf16[1,1,384,512]{2,3,1,0:T(8,128)(2,1)S(1)}, bf16[1,1,384,512]{2,3,1,0:T(8,128)(2,1)}, u32[]{:S(2)}) copy-start(bf16[1,1,384,512]{2,3,1,0:T(8,128)(2,1)} %copy.76) | copy-start | bytes 1179652
  161.2 11.6 %copy-start.31 = (bf16[384,512]{0,1:T(8,128)(2,1)S(1)}, bf16[384,512]{0,1:T(8,128)(2,1)}, u32[]{:S(2)}) copy-start(bf16[384,512]{0,1:T(8,128)(2,1)} %copy.73) | copy-start | bytes 1179652
  161.2 11.6 %copy-start.32 = (bf16[384,512]{0,1:T(8,128)(2,1)S(1)}, bf16[384,512]{0,1:T(8,128)(2,1)}, u32[]{:S(2)}) copy-start(bf16[384,512]{0,1:T(8,128)(2,1)} %copy.74) | copy-start | bytes 1179652
  172.8 13.4 %copy-start.4 = (bf16[1,1,512,512]{2,3,1,0:T(8,128)(2,1)S(1)}, bf16[1,1,512,512]{2,3,1,0:T(8,128)(2,1)}, u32[]{:S(2)}) copy-start(bf16[1,1,512,512]{2,3,1,0:T(8,128)(2,1)} %copy.134) | copy-start | bytes 1572868
  186.2 17.7 %copy-start.11 = (bf16[384,512]{0,1:T(8,128)(2,1)S(1)}, bf16[384,512]{0,1:T(8,128)(2,1)}, u32[]{:S(2)}) copy-start(bf16[384,512]{0,1:T(8,128)(2,1)} %get-tuple-element.36) | copy-start | bytes 1179652
  188.5 18.5 %copy-start.12 = (bf16[384,512]{1,0:T(8,128)(2,1)S(1)}, bf16[384,512]{1,0:T(8,128)(2,1)}, u32[]{:S(2)}) copy-start(bf16[384,512]{1,0:T(8,128)(2,1)} %get-tuple-element.122) | copy-start | bytes 1179652
  215.8 7.4 %copy-start.13 = (pred[4,128,384]{1,2,0:T(8,128)(4,1)S(1)}, pred[4,128,384]{1,2,0:T(8,128)(4,1)}, u32[]{:S(2)}) copy-start(pred[4,128,384]{1,2,0:T(8,128)(4,1)} %get-tuple-element.46) | copy-start | bytes 589828
  215.8 7.4 %copy-start.19 = (bf16[1,384,4,128]{3,1,2,0:T(8,128)(2,1)S(1)}, bf16[1,384,4,128]{3,1,2,0:T(8,128)(2,1)}, u32[]{:S(2)}) copy-start(bf16[1,384,4,128]{3,1,2,0:T(8,128)(2,1)} %copy.105) | copy-start | bytes 1179652
  215.8 7.4 %copy-start.20 = (bf16[1,384,4,128]{3,1,2,0:T(8,128)(2,1)S(1)}, bf16[1,384,4,128]{3,1,2,0:T(8,128)(2,1)}, u32[]{:S(2)}) copy-start(bf16[1,384,4,128]{3,1,2,0:T(8,128)(2,1)} %copy.106) | copy-start | bytes 1179652
  255.5 27.6 %collective-permute-start.5 = (bf16[256,4096]{1,0:T(8,128)(2,1)}, bf16[256,4096]{1,0:T(8,128)(2,1)S(1)}, u32[]{:S(2)}, u32[]{:S(2)}) collective-permute-start(bf16[256,4096]{1,0:T(8,128)(2,1)} %reshape.521), channel_id=1, source_target_pairs={{0,1},{1,2},{2,3},{3,4},{4,5},{5,6},{6,7},{7,8},{8,9},{9,10},{10,1... | collective-permute-start | bytes 6291464 | tf_op jit(solution)/shard_map/ppermute | solution.py:21
  272.1 11.0 %copy-start.1 = (bf16[512,4096]{1,0:T(8,128)(2,1)S(1)}, bf16[512,4096]{1,0:T(8,128)(2,1)}, u32[]{:S(2)}) copy-start(bf16[512,4096]{1,0:T(8,128)(2,1)} %reshape.519) | copy-start | bytes 12582916
  272.1 11.0 %copy-start.51 = (pred[512]{0:T(512)(128)(4,1)S(1)}, pred[512]{0:T(512)(128)(4,1)}, u32[]{:S(2)}) copy-start(pred[512]{0:T(512)(128)(4,1)} %broadcast_bitcast_fusion.11) | copy-start | bytes 1540
  287.1 94.0 %collective-permute-start.13 = (bf16[512,4096]{1,0:T(8,128)(2,1)}, bf16[512,4096]{1,0:T(8,128)(2,1)}, u32[]{:S(2)}, u32[]{:S(2)}) collective-permute-start(bf16[512,4096]{1,0:T(8,128)(2,1)} %pad_select_fusion.1), channel_id=1, source_target_pairs={{32,0},{64,32},{96,64},{33,1},{65,33},{97,65},{34,2},{66,34},{98,6... | collective-permute-start | bytes 12582920 | tf_op jit(solution)/shard_map/ppermute | solution.py:21
  297.7 8.0 %copy-start.17 = (bf16[1,1,384,512]{2,3,1,0:T(8,128)(2,1)S(1)}, bf16[1,1,384,512]{2,3,1,0:T(8,128)(2,1)}, u32[]{:S(2)}) copy-start(bf16[1,1,384,512]{2,3,1,0:T(8,128)(2,1)} %copy.98) | copy-start | bytes 1179652
  297.7 8.0 %copy-start.18 = (bf16[1,1,384,512]{2,3,1,0:T(8,128)(2,1)S(1)}, bf16[1,1,384,512]{2,3,1,0:T(8,128)(2,1)}, u32[]{:S(2)}) copy-start(bf16[1,1,384,512]{2,3,1,0:T(8,128)(2,1)} %copy.99) | copy-start | bytes 1179652
  297.7 8.0 %copy-start.23 = (bf16[384,512]{0,1:T(8,128)(2,1)S(1)}, bf16[384,512]{0,1:T(8,128)(2,1)}, u32[]{:S(2)}) copy-start(bf16[384,512]{0,1:T(8,128)(2,1)} %copy.96) | copy-start | bytes 1179652
  303.5 30.4 %collective-permute-start.11 = (bf16[256,4096]{1,0:T(8,128)(2,1)}, bf16[256,4096]{1,0:T(8,128)(2,1)S(1)}, u32[]{:S(2)}, u32[]{:S(2)}) collective-permute-start(bf16[256,4096]{1,0:T(8,128)(2,1)} %reshape.528), channel_id=1, source_target_pairs={{0,1},{1,2},{2,3},{3,4},{4,5},{5,6},{6,7},{7,8},{8,9},{9,10},{10,1... | collective-permute-start | bytes 6291464 | tf_op jit(solution)/shard_map/ppermute | solution.py:21
  326.7 54.5 %copy-start.48 = (pred[512]{0:T(512)(128)(4,1)S(1)}, pred[512]{0:T(512)(128)(4,1)}, u32[]{:S(2)}) copy-start(pred[512]{0:T(512)(128)(4,1)} %broadcast_bitcast_fusion.10) | copy-start | bytes 1540
  389.6 93.2 %collective-permute-start.12 = (bf16[512,4096]{1,0:T(8,128)(2,1)}, bf16[512,4096]{1,0:T(8,128)(2,1)}, u32[]{:S(2)}, u32[]{:S(2)}) collective-permute-start(bf16[512,4096]{1,0:T(8,128)(2,1)} %get-tuple-element.9), channel_id=1, source_target_pairs={{0,32},{32,64},{64,96},{1,33},{33,65},{65,97},{2,34},{34,66},{66,9... | collective-permute-start | bytes 12582920 | tf_op jit(solution)/shard_map/ppermute | solution.py:21
  (18 other events, 74.0 us)
where the time goes:
time: 497 us; the launch traced here: 488 us
  waiting for transfers between devices  168 us (34%)
  local copies, waits for them, and re-layouts  140 us (28%)
  other arithmetic  73.4 us (15%)
  matrix products  70.4 us (14%)
  starting transfers between devices  34.7 us (7%)
    ppermute x14, waiting for transfers between devices, shifted(): lax.ppermute(value, axis, [(source, source + steps) for source in range(i...  168 us
    dot_general x4, matrix products, attend(): jnp.einsum('ahgqk,akhd->aqhgd', rounded, valueset, preferred_element_type...  35.8 us
    ppermute x14, starting transfers between devices, shifted(): lax.ppermute(value, axis, [(source, source + steps) for source in range(i...  34.7 us
    dot_general x4, matrix products, attend(): jnp.einsum('aqhgd,akhd->ahgqk', query, keyset, preferred_element_type=jnp...  34.6 us
    reduce_sum x4, other arithmetic, attend(): totals = jnp.sum(weights, axis=-1)  30.9 us
    unnamed x133, local copies, waits for them, and re-layouts  30.4 us
    another operation x40, local copies, waits for them, and re-layouts, windowed(): jnp.stack([lax.slice_in_dim(rows, (index + offset) * BLK, (index + offset...  28.5 us
    convert_element_type x4, local copies, waits for them, and re-layouts, attend(): (mixed / totals).astype(jnp.bfloat16).reshape(group_count * BLK, -1)  22.7 us
  transfers between devices with their start and end apart: 14, of which 4 were waited for; matrix products, arithmetic and copies ran while one was open for 54% of the time, Pallas kernels for 0%

commit v1 on v0

v1 whole, which is shorter than its diff:
```python
import functools
import math

import jax
import jax.numpy as jnp
from jax import lax
from jax.experimental import pallas as pl
from jax.experimental.pallas import tpu as pltpu
from jax.sharding import PartitionSpec as P

BLK = 128
TREE_MOST = 3
KV_HEADS = 4
GROUP = 8
HEAD = 128
ROWS = 512
BLOCKS = ROWS // BLK
REACH = (TREE_MOST - 1) * BLK
SPAN = TREE_MOST * BLK
WIDE = GROUP * HEAD
STEPS = BLOCKS * KV_HEADS

NEG = -1e30
MESH = pl.DeviceIdType.MESH


def kernel(
    queries, keys, values, segment, parent,
    forward, returned,
    qbuf, kbuf, vbuf, segbuf, parbuf, bias, stage,
    qsem, ownsem, halo_send, halo_recv, send, land_forward, land_returned,
):
    n_pipe, n_dp = lax.axis_size("pipe"), lax.axis_size("dp")
    place, me = lax.axis_index("pipe"), lax.axis_index("dp")
    after, before = lax.rem(me + 1, n_dp), lax.rem(me + n_dp - 1, n_dp)
    up, down = lax.rem(place + 1, n_pipe), lax.rem(place + n_pipe - 1, n_pipe)

    barrier = pltpu.get_barrier_semaphore()
    for target in ((place, after), (place, before), (up, me), (down, me)):
        pl.semaphore_signal(barrier, inc=1, device_id=target, device_id_type=MESH)

    own = [
        pltpu.make_async_copy(source, target, ownsem.at[index])
        for index, (source, target) in enumerate(
            (
                (segment, segbuf.at[:, pl.ds(REACH, ROWS)]),
                (parent, parbuf.at[:, pl.ds(REACH, ROWS)]),
                (keys, kbuf.at[:, pl.ds(REACH, ROWS)]),
                (values, vbuf.at[:, pl.ds(REACH, ROWS)]),
            )
        )
    ]
    for copy in own:
        copy.start()

    def place_of(step):
        block = lax.rem(step // KV_HEADS + (TREE_MOST - 1), BLOCKS)
        head = lax.rem(step, KV_HEADS)
        return (
            block,
            head,
            pl.ds(pl.multiple_of(block * BLK, BLK), BLK),
            pl.ds(pl.multiple_of(head * WIDE, WIDE), WIDE),
        )

    def query_copy(step):
        _, _, rows, columns = place_of(step)
        return pltpu.make_async_copy(
            queries.at[:, rows, columns], qbuf.at[:, rows, columns], qsem.at[step]
        )

    @pl.loop(0, STEPS)
    def _(step):
        query_copy(step).start()

    pl.semaphore_wait(barrier, 4)
    tail = pl.ds(ROWS - REACH, REACH)
    halo = [
        pltpu.make_async_remote_copy(
            src_ref=source,
            dst_ref=target,
            send_sem=halo_send.at[index],
            recv_sem=halo_recv.at[index],
            device_id=(place, after),
            device_id_type=MESH,
        )
        for index, (source, target) in enumerate(
            (
                (segment.at[:, tail], segbuf.at[:, pl.ds(0, REACH)]),
                (parent.at[:, tail], parbuf.at[:, pl.ds(0, REACH)]),
                (keys.at[:, tail], kbuf.at[:, pl.ds(0, REACH)]),
                (values.at[:, tail], vbuf.at[:, pl.ds(0, REACH)]),
            )
        )
    ]
    for copy in halo:
        copy.start()

    def row_of(ref, path, window_block):
        row = ref[path : path + 1, window_block * BLK : (window_block + 1) * BLK]
        return row.astype(jnp.float32)

    def build_bias(path, block):
        later = lax.broadcasted_iota(jnp.int32, (BLK, BLK), 1) <= lax.broadcasted_iota(
            jnp.int32, (BLK, BLK), 0
        )
        segs = [row_of(segbuf, path, block + index) for index in range(TREE_MOST)]
        pars = [row_of(parbuf, path, block + index) for index in range(TREE_MOST)]
        first = jnp.full((1, BLK), -1.0, jnp.float32)
        for index in range(TREE_MOST):
            opening = jnp.where(segs[index] == pars[index], segs[index], -1.0)
            if block + index < TREE_MOST - 1:
                opening = jnp.where(me > 0, opening, -1.0)
            first = jnp.maximum(first, opening)
        root = jnp.broadcast_to(jnp.max(first, axis=1, keepdims=True), (BLK, BLK))
        own_seg = jnp.broadcast_to(segs[-1], (BLK, BLK)).T
        own_par = jnp.broadcast_to(pars[-1], (BLK, BLK)).T
        for index in range(TREE_MOST):
            other = jnp.broadcast_to(segs[index], (BLK, BLK))
            allowed = (other == own_seg) | (other == own_par) | (other == root)
            if index == TREE_MOST - 1:
                allowed = allowed & later
            bias[path * BLOCKS + block, :, index * BLK : (index + 1) * BLK] = jnp.where(
                allowed, 0.0, NEG
            )

    scale = math.log2(math.e) / math.sqrt(HEAD)

    def attend(path, block, head, rows, columns):
        window = pl.ds(pl.multiple_of(block * BLK, BLK), SPAN)
        lanes = pl.ds(pl.multiple_of(head * HEAD, HEAD), HEAD)
        key = kbuf[path, window, lanes]
        value = vbuf[path, window, lanes]
        mask = bias[path * BLOCKS + block]
        for member in range(GROUP):
            part = pl.ds(pl.multiple_of(head * WIDE + member * HEAD, HEAD), HEAD)
            query = qbuf[path, rows, part]
            scores = lax.dot_general(
                query, key, (((1,), (1,)), ((), ())), preferred_element_type=jnp.float32
            )
            scores = scores * scale + mask
            top = jnp.max(scores, axis=1, keepdims=True)
            weights = jnp.exp2(scores - top)
            totals = jnp.sum(weights, axis=1, keepdims=True)
            mixed = jnp.dot(
                weights.astype(jnp.bfloat16), value, preferred_element_type=jnp.float32
            )
            stage[path, rows, part] = (mixed / totals).astype(jnp.bfloat16)

    def away(path, step):
        _, _, rows, columns = place_of(step)
        target, landed, to = (
            (forward, land_forward, up) if path == 0 else (returned, land_returned, down)
        )
        return pltpu.make_async_remote_copy(
            src_ref=stage.at[path, rows, columns],
            dst_ref=target.at[rows, columns],
            send_sem=send.at[path, step],
            recv_sem=landed.at[step],
            device_id=(to, me),
            device_id_type=MESH,
        )

    def stay(path, step):
        _, _, rows, columns = place_of(step)
        target, landed = (
            (returned, land_returned) if path == 0 else (forward, land_forward)
        )
        return pltpu.make_async_copy(
            stage.at[path, rows, columns], target.at[rows, columns], landed.at[step]
        )

    edges = (n_pipe - 1, 0)

    def work(step):
        block, head, rows, columns = place_of(step)
        query_copy(step).wait()
        for path in range(2):
            attend(path, block, head, rows, columns)

            @pl.when(place != edges[path])
            def _():
                away(path, step).start()

            @pl.when(place == edges[path])
            def _():
                stay(path, step).start()

    for copy in own:
        copy.wait()
    for path in range(2):
        for block in range(TREE_MOST - 1, BLOCKS):
            build_bias(path, block)
    half = (BLOCKS - TREE_MOST + 1) * KV_HEADS
    pl.loop(0, half)(work)
    for copy in halo:
        copy.wait()
    for path in range(2):
        for block in range(TREE_MOST - 1):
            build_bias(path, block)
    pl.loop(half, STEPS)(work)

    @pl.loop(0, STEPS)
    def _(step):
        for path in range(2):

            @pl.when(place != edges[path])
            def _():
                away(path, step).wait_send()

            @pl.when(place != edges[1 - path])
            def _():
                away(path, step).wait_recv()

            @pl.when(place == edges[path])
            def _():
                stay(path, step).wait()


def on_device(queries, keys, values, segment, parent, tree_lengths):
    hbm = pl.BlockSpec(memory_space=pl.ANY)
    width = KV_HEADS * GROUP * HEAD
    narrow = KV_HEADS * HEAD
    out = jax.ShapeDtypeStruct((ROWS, width), jnp.bfloat16)
    forward, returned = pl.pallas_call(
        kernel,
        out_shape=(out, out),
        in_specs=[hbm] * 5,
        out_specs=[hbm] * 2,
        scratch_shapes=[
            pltpu.VMEM((2, ROWS, width), jnp.bfloat16),
            pltpu.VMEM((2, REACH + ROWS, narrow), jnp.bfloat16),
            pltpu.VMEM((2, REACH + ROWS, narrow), jnp.bfloat16),
            pltpu.VMEM((2, REACH + ROWS), jnp.int32),
            pltpu.VMEM((2, REACH + ROWS), jnp.int32),
            pltpu.VMEM((2 * BLOCKS, BLK, SPAN), jnp.float32),
            pltpu.VMEM((2, ROWS, width), jnp.bfloat16),
            pltpu.SemaphoreType.DMA((STEPS,)),
            pltpu.SemaphoreType.DMA((4,)),
            pltpu.SemaphoreType.DMA((4,)),
            pltpu.SemaphoreType.DMA((4,)),
            pltpu.SemaphoreType.DMA((2, STEPS)),
            pltpu.SemaphoreType.DMA((STEPS,)),
            pltpu.SemaphoreType.DMA((STEPS,)),
        ],
        compiler_params=pltpu.CompilerParams(
            collective_id=0, has_side_effects=True, vmem_limit_bytes=40 << 20
        ),
        name="relay",
    )(queries[0], keys[0], values[0], segment[0], parent[0])
    return (forward[None], returned[None])


def solution(mesh):
    return jax.shard_map(
        on_device,
        mesh=mesh,
        in_specs=(
            P("pipe", None, "dp", None),
            P("pipe", None, "dp", None),
            P("pipe", None, "dp", None),
            P("pipe", None, "dp"),
            P("pipe", None, "dp"),
            P("pipe", None, None),
        ),
        out_specs=(P("pipe", "dp", None), P("pipe", "dp", None)),
        check_vma=False,
    )
```

time: 497 us -> 110 us (0.22)
  the two profiles are of different devices: /device:TPU:54 before, /device:TPU:0 now
where the time goes in v1:
time: 110 us
  Pallas kernels  102 us (93%)
  local copies, waits for them, and re-layouts  7.84 us (7%)
    pallas_call x1, Pallas kernels, on_device(): pl.pallas_call(kernel, out_shape=(out, out), in_specs=[hbm] * 5, out_spec...  102 us
    unnamed x10, local copies, waits for them, and re-layouts  7.84 us

profile of v1, /device:TPU:0, one launch (start us, length us, event | category | flops | bytes accessed | tf_op | source)
XLA Modules:
  0.0 110.0 jit_solution(3338583243013424327)
XLA Ops:
  0.6 0.0 copy-start
  0.6 1.2 %copy-done = bf16[1,2,512,512]{3,2,1,0:T(8,128)(2,1)S(1)} copy-done((bf16[1,2,512,512]{3,2,1,0:T(8,128)(2,1)S(1)}, bf16[1,2,512,512]{3,2,1,0:T(8,128)(2,1)}, u32[]{:S(2)}) %copy-start) | copy-done | bytes 1048600
  1.9 0.0 copy-start.1
  1.9 1.2 %copy-done.1 = bf16[1,2,512,512]{3,2,1,0:T(8,128)(2,1)S(1)} copy-done((bf16[1,2,512,512]{3,2,1,0:T(8,128)(2,1)S(1)}, bf16[1,2,512,512]{3,2,1,0:T(8,128)(2,1)}, u32[]{:S(2)}) %copy-start.1) | copy-done | bytes 1048600
  3.1 0.0 copy-start.2
  3.1 0.7 copy-done.2
  3.8 0.0 copy-start.3
  3.8 0.7 copy-done.3
  4.5 101.5 %relay.1 = (bf16[512,4096]{1,0:T(8,128)(2,1)S(1)}, bf16[512,4096]{1,0:T(8,128)(2,1)S(1)}) custom-call(bf16[2,512,4096]{2,1,0:T(8,128)(2,1)} %bitcast.13, bf16[2,512,512]{2,1,0:T(8,128)(2,1)S(1)} %bitcast.9, bf16[2,512,512]{2,1,0:T(8,128)(2,1)S(1)} %bitcast.10, s32[2,512]{1,0:T(2,128)S(1)} %bitcast.11, s32[2,512]{1,0:T(2,128)S(1)} %bitcast.12), custom_call_target="tpu_custom_call" | custom-call | tf_op jit(solution)/shard_map/relay/pallas_call | solution.py:225
  106.0 2.0 %copy.9 = bf16[1,512,4096]{2,1,0:T(8,128)(2,1)} copy(bf16[1,512,4096]{2,1,0:T(8,128)(2,1)S(1)} %bitcast.8) | data formatting | bytes 8388608
  108.0 2.0 %copy.10 = bf16[1,512,4096]{2,1,0:T(8,128)(2,1)} copy(bf16[1,512,4096]{2,1,0:T(8,128)(2,1)S(1)} %bitcast.7) | data formatting | bytes 8388608
Async XLA Ops:
  0.6 1.2 %copy-start = (bf16[1,2,512,512]{3,2,1,0:T(8,128)(2,1)S(1)}, bf16[1,2,512,512]{3,2,1,0:T(8,128)(2,1)}, u32[]{:S(2)}) copy-start(bf16[1,2,512,512]{3,2,1,0:T(8,128)(2,1)} %param.7) | copy-start | bytes 3145732
  1.9 1.2 %copy-start.1 = (bf16[1,2,512,512]{3,2,1,0:T(8,128)(2,1)S(1)}, bf16[1,2,512,512]{3,2,1,0:T(8,128)(2,1)}, u32[]{:S(2)}) copy-start(bf16[1,2,512,512]{3,2,1,0:T(8,128)(2,1)} %param.8) | copy-start | bytes 3145732
  3.1 0.7 copy-start.2
  3.8 0.7 copy-start.3

commit v2 on v1

v2 whole, which is shorter than its diff:
```python
import functools
import math

import jax
import jax.numpy as jnp
from jax import lax
from jax.experimental import pallas as pl
from jax.experimental.pallas import tpu as pltpu
from jax.sharding import PartitionSpec as P

BLK = 128
TREE_MOST = 3
KV_HEADS = 4
GROUP = 8
HEAD = 128
ROWS = 512
BLOCKS = ROWS // BLK
REACH = (TREE_MOST - 1) * BLK
SPAN = TREE_MOST * BLK
WIDE = GROUP * HEAD
STEPS = BLOCKS * KV_HEADS
AHEAD = 3

NEG = -1e30
MESH = pl.DeviceIdType.MESH


def kernel(
    queries, keys, values, segment, parent,
    forward, returned,
    qbuf, kbuf, vbuf, segbuf, parbuf, bias, stage,
    qsem, infosem, ownsem, halo_send, halo_recv, send, land_forward, land_returned,
):
    n_pipe, n_dp = lax.axis_size("pipe"), lax.axis_size("dp")
    place, me = lax.axis_index("pipe"), lax.axis_index("dp")
    after, before = lax.rem(me + 1, n_dp), lax.rem(me + n_dp - 1, n_dp)
    up, down = lax.rem(place + 1, n_pipe), lax.rem(place + n_pipe - 1, n_pipe)

    barrier = pltpu.get_barrier_semaphore()
    for target in ((place, after), (place, before), (up, me), (down, me)):
        pl.semaphore_signal(barrier, inc=1, device_id=target, device_id_type=MESH)

    def place_of(step):
        block = lax.rem(step // KV_HEADS + (TREE_MOST - 1), BLOCKS)
        head = lax.rem(step, KV_HEADS)
        return (
            block,
            head,
            pl.ds(pl.multiple_of(block * BLK, BLK), BLK),
            pl.ds(pl.multiple_of(head * WIDE, WIDE), WIDE),
        )

    def query_copy(step):
        _, _, rows, columns = place_of(step)
        return pltpu.make_async_copy(
            queries.at[:, rows, columns], qbuf.at[:, rows, columns], qsem.at[step]
        )

    def own_copy(index, head):
        source, target = ((keys, kbuf), (values, vbuf))[index]
        lanes = pl.ds(head * HEAD, HEAD)
        return pltpu.make_async_copy(
            source.at[:, :, lanes],
            target.at[:, pl.ds(REACH, ROWS), lanes],
            ownsem.at[index, head],
        )

    infos = [
        pltpu.make_async_copy(source, target.at[:, pl.ds(REACH, ROWS)], infosem.at[index])
        for index, (source, target) in enumerate(((segment, segbuf), (parent, parbuf)))
    ]
    for copy in infos:
        copy.start()
    own_copy(0, 0).start()
    query_copy(0).start()
    own_copy(1, 0).start()
    for head in range(1, KV_HEADS):
        own_copy(0, head).start()
        own_copy(1, head).start()
    for step in range(1, AHEAD):
        query_copy(step).start()

    tail = pl.ds(ROWS - REACH, REACH)
    halo = [
        pltpu.make_async_remote_copy(
            src_ref=source.at[:, tail],
            dst_ref=target.at[:, pl.ds(0, REACH)],
            send_sem=halo_send.at[index],
            recv_sem=halo_recv.at[index],
            device_id=(place, after),
            device_id_type=MESH,
        )
        for index, (source, target) in enumerate(
            ((segment, segbuf), (parent, parbuf), (keys, kbuf), (values, vbuf))
        )
    ]

    def row_of(ref, path, window_block):
        row = ref[path : path + 1, window_block * BLK : (window_block + 1) * BLK]
        return row.astype(jnp.float32)

    def build_bias(path, block):
        later = lax.broadcasted_iota(jnp.int32, (BLK, BLK), 1) <= lax.broadcasted_iota(
            jnp.int32, (BLK, BLK), 0
        )
        segs = [row_of(segbuf, path, block + index) for index in range(TREE_MOST)]
        pars = [row_of(parbuf, path, block + index) for index in range(TREE_MOST)]
        first = jnp.full((1, BLK), -1.0, jnp.float32)
        for index in range(TREE_MOST):
            opening = jnp.where(segs[index] == pars[index], segs[index], -1.0)
            if block + index < TREE_MOST - 1:
                opening = jnp.where(me > 0, opening, -1.0)
            first = jnp.maximum(first, opening)
        root = jnp.broadcast_to(jnp.max(first, axis=1, keepdims=True), (BLK, BLK))
        own_seg = jnp.broadcast_to(segs[-1], (BLK, BLK)).T
        own_par = jnp.broadcast_to(pars[-1], (BLK, BLK)).T
        for index in range(TREE_MOST):
            other = jnp.broadcast_to(segs[index], (BLK, BLK))
            allowed = (other == own_seg) | (other == own_par) | (other == root)
            if index == TREE_MOST - 1:
                allowed = allowed & later
            bias[path * BLOCKS + block, :, index * BLK : (index + 1) * BLK] = jnp.where(
                allowed, 0.0, NEG
            )

    scale = math.log2(math.e) / math.sqrt(HEAD)

    def attend(path, step, members):
        block, head, rows, _ = place_of(step)
        window = pl.ds(pl.multiple_of(block * BLK, BLK), SPAN)
        lanes = pl.ds(pl.multiple_of(head * HEAD, HEAD), HEAD)
        key = kbuf[path, window, lanes]
        value = vbuf[path, window, lanes]
        mask = bias[path * BLOCKS + block]
        parts = [
            pl.ds(pl.multiple_of(head * WIDE + member * HEAD, HEAD), HEAD) for member in members
        ]
        query = jnp.concatenate([qbuf[path, rows, part] for part in parts], axis=0)
        scores = lax.dot_general(
            query, key, (((1,), (1,)), ((), ())), preferred_element_type=jnp.float32
        )
        weights, totals = [], []
        for index in range(len(members)):
            score = scores[index * BLK : (index + 1) * BLK] * scale + mask
            weight = jnp.exp2(score - jnp.max(score, axis=1, keepdims=True))
            totals.append(jnp.sum(weight, axis=1, keepdims=True))
            weights.append(weight.astype(jnp.bfloat16))
        mixed = jnp.dot(
            jnp.concatenate(weights, axis=0), value, preferred_element_type=jnp.float32
        )
        for index, part in enumerate(parts):
            result = mixed[index * BLK : (index + 1) * BLK] / totals[index]
            stage[path, rows, part] = result.astype(jnp.bfloat16)

    def region(step, members):
        _, head, rows, _ = place_of(step)
        start = pl.multiple_of(head * WIDE + members[0] * HEAD, HEAD)
        return rows, pl.ds(start, len(members) * HEAD)

    def away(path, step, members):
        rows, columns = region(step, members)
        target, landed, to = (
            (forward, land_forward, up) if path == 0 else (returned, land_returned, down)
        )
        return pltpu.make_async_remote_copy(
            src_ref=stage.at[path, rows, columns],
            dst_ref=target.at[rows, columns],
            send_sem=send.at[path, step],
            recv_sem=landed.at[step],
            device_id=(to, me),
            device_id_type=MESH,
        )

    def stay(path, step, members):
        rows, columns = region(step, members)
        target, landed = (
            (returned, land_returned) if path == 0 else (forward, land_forward)
        )
        return pltpu.make_async_copy(
            stage.at[path, rows, columns], target.at[rows, columns], landed.at[step]
        )

    edges = (n_pipe - 1, 0)
    every = tuple(range(GROUP))

    def leave(path, step, members):
        @pl.when(place != edges[path])
        def _():
            away(path, step, members).start()

        @pl.when(place == edges[path])
        def _():
            stay(path, step, members).start()

    def fetch(step):
        @pl.when(step + AHEAD < STEPS)
        def _():
            query_copy(step + AHEAD).start()

        query_copy(step).wait()

    def work(step):
        fetch(step)
        for path in range(2):
            attend(path, step, every)
            leave(path, step, every)

    for copy in infos:
        copy.wait()
    for path in range(2):
        build_bias(path, TREE_MOST - 1)
    pl.semaphore_wait(barrier, 4)
    for copy in halo:
        copy.start()
    own_copy(0, 0).wait()
    own_copy(1, 0).wait()
    fetch(0)
    for members in ((0,), (1,), (2, 3), (4, 5, 6, 7)):
        for path in range(2):
            attend(path, 0, members)
        for path in range(2):
            leave(path, 0, members)
    for head in range(1, KV_HEADS):
        own_copy(0, head).wait()
        own_copy(1, head).wait()
    pl.loop(1, KV_HEADS)(work)
    for block in range(TREE_MOST, BLOCKS):
        for path in range(2):
            build_bias(path, block)
    half = (BLOCKS - TREE_MOST + 1) * KV_HEADS
    pl.loop(KV_HEADS, half)(work)
    for copy in halo:
        copy.wait()
    for block in range(TREE_MOST - 1):
        for path in range(2):
            build_bias(path, block)
    pl.loop(half, STEPS)(work)

    @pl.loop(0, STEPS)
    def _(step):
        for path in range(2):

            @pl.when(place != edges[path])
            def _():
                away(path, step, every).wait_send()

            @pl.when(place != edges[1 - path])
            def _():
                away(path, step, every).wait_recv()

            @pl.when(place == edges[path])
            def _():
                stay(path, step, every).wait()


def on_device(queries, keys, values, segment, parent, tree_lengths):
    width = KV_HEADS * GROUP * HEAD
    narrow = KV_HEADS * HEAD
    out = jax.ShapeDtypeStruct((ROWS, width), jnp.bfloat16)
    forward, returned = pl.pallas_call(
        kernel,
        out_shape=(out, out),
        in_specs=[pl.BlockSpec(memory_space=pltpu.HBM)] * 5,
        out_specs=[pl.BlockSpec(memory_space=pl.ANY)] * 2,
        scratch_shapes=[
            pltpu.VMEM((2, ROWS, width), jnp.bfloat16),
            pltpu.VMEM((2, REACH + ROWS, narrow), jnp.bfloat16),
            pltpu.VMEM((2, REACH + ROWS, narrow), jnp.bfloat16),
            pltpu.VMEM((2, REACH + ROWS), jnp.int32),
            pltpu.VMEM((2, REACH + ROWS), jnp.int32),
            pltpu.VMEM((2 * BLOCKS, BLK, SPAN), jnp.float32),
            pltpu.VMEM((2, ROWS, width), jnp.bfloat16),
            pltpu.SemaphoreType.DMA((STEPS,)),
            pltpu.SemaphoreType.DMA((2,)),
            pltpu.SemaphoreType.DMA((2, KV_HEADS)),
            pltpu.SemaphoreType.DMA((4,)),
            pltpu.SemaphoreType.DMA((4,)),
            pltpu.SemaphoreType.DMA((2, STEPS)),
            pltpu.SemaphoreType.DMA((STEPS,)),
            pltpu.SemaphoreType.DMA((STEPS,)),
        ],
        compiler_params=pltpu.CompilerParams(
            collective_id=0, has_side_effects=True, vmem_limit_bytes=40 << 20
        ),
        name="relay",
    )(*[pltpu.with_memory_space_constraint(x[0], pltpu.HBM) for x in (queries, keys, values, segment, parent)])
    return (forward[None], returned[None])


def solution(mesh):
    return jax.shard_map(
        on_device,
        mesh=mesh,
        in_specs=(
            P("pipe", None, "dp", None),
            P("pipe", None, "dp", None),
            P("pipe", None, "dp", None),
            P("pipe", None, "dp"),
            P("pipe", None, "dp"),
            P("pipe", None, None),
        ),
        out_specs=(P("pipe", "dp", None), P("pipe", "dp", None)),
        check_vma=False,
    )
```

time: 110 us -> 102 us (0.927)
  Pallas kernels: 102 us -> 97.1 us
  local copies, waits for them, and re-layouts: 7.84 us -> 4.03 us
    pallas_call x1, Pallas kernels: 102 us -> 97.1 us  [on_device(): pl.pallas_call(kernel, out_shape=(out, out), in_specs=[pl.BlockSpec(memor...]
    unnamed x10 -> x2, local copies, waits for them, and re-layouts: 7.84 us -> 4.03 us
where the time goes in v2:
time: 102 us
  Pallas kernels  97.1 us (95%)
  local copies, waits for them, and re-layouts  4.03 us (4%)
    pallas_call x1, Pallas kernels, on_device(): pl.pallas_call(kernel, out_shape=(out, out), in_specs=[pl.BlockSpec(memor...  97.1 us
    unnamed x2, local copies, waits for them, and re-layouts  4.03 us

profile of v2, /device:TPU:0, one launch (start us, length us, event | category | flops | bytes accessed | tf_op | source)
XLA Modules:
  0.0 101.8 jit_solution(13521257051457614538)
XLA Ops:
  0.6 97.1 %relay.1 = (bf16[512,4096]{1,0:T(8,128)(2,1)S(1)}, bf16[512,4096]{1,0:T(8,128)(2,1)S(1)}) custom-call(bf16[2,512,4096]{2,1,0:T(8,128)(2,1)} %bitcast.9, bf16[2,512,512]{2,1,0:T(8,128)(2,1)} %bitcast.10, bf16[2,512,512]{2,1,0:T(8,128)(2,1)} %bitcast.11, s32[2,512]{1,0:T(2,128)} %bitcast.12, s32[2,512]{1,0:T(2,128)} %bitcast.13), custom_call_target="tpu_custom_call" | custom-call | tf_op jit(solution)/shard_map/relay/pallas_call | solution.py:260
  97.8 2.0 %copy.9 = bf16[1,512,4096]{2,1,0:T(8,128)(2,1)} copy(bf16[1,512,4096]{2,1,0:T(8,128)(2,1)S(1)} %bitcast.8) | data formatting | bytes 8388608
  99.8 2.0 %copy.10 = bf16[1,512,4096]{2,1,0:T(8,128)(2,1)} copy(bf16[1,512,4096]{2,1,0:T(8,128)(2,1)S(1)} %bitcast.7) | data formatting | bytes 8388608

commit v3 on v2

--- a/solution.py
+++ b/solution.py
@@ -20,6 +20,7 @@
 WIDE = GROUP * HEAD
 STEPS = BLOCKS * KV_HEADS
 AHEAD = 3
+PIECES = 2
 
 NEG = -1e30
 MESH = pl.DeviceIdType.MESH
@@ -36,10 +37,6 @@
     after, before = lax.rem(me + 1, n_dp), lax.rem(me + n_dp - 1, n_dp)
     up, down = lax.rem(place + 1, n_pipe), lax.rem(place + n_pipe - 1, n_pipe)
 
-    barrier = pltpu.get_barrier_semaphore()
-    for target in ((place, after), (place, before), (up, me), (down, me)):
-        pl.semaphore_signal(barrier, inc=1, device_id=target, device_id_type=MESH)
-
     def place_of(step):
         block = lax.rem(step // KV_HEADS + (TREE_MOST - 1), BLOCKS)
         head = lax.rem(step, KV_HEADS)
@@ -69,17 +66,6 @@
         pltpu.make_async_copy(source, target.at[:, pl.ds(REACH, ROWS)], infosem.at[index])
         for index, (source, target) in enumerate(((segment, segbuf), (parent, parbuf)))
     ]
-    for copy in infos:
-        copy.start()
-    own_copy(0, 0).start()
-    query_copy(0).start()
-    own_copy(1, 0).start()
-    for head in range(1, KV_HEADS):
-        own_copy(0, head).start()
-        own_copy(1, head).start()
-    for step in range(1, AHEAD):
-        query_copy(step).start()
-
     tail = pl.ds(ROWS - REACH, REACH)
     halo = [
         pltpu.make_async_remote_copy(
@@ -154,6 +140,8 @@
 
     def region(step, members):
         _, head, rows, _ = place_of(step)
+        if members is None:
+            return rows, slice(None)
         start = pl.multiple_of(head * WIDE + members[0] * HEAD, HEAD)
         return rows, pl.ds(start, len(members) * HEAD)
 
@@ -203,23 +191,45 @@
         fetch(step)
         for path in range(2):
             attend(path, step, every)
-            leave(path, step, every)
-
+
+            @pl.when(step < KV_HEADS)
+            def _():
+                leave(path, step, every)
+
+            @pl.when((step >= KV_HEADS) & (lax.rem(step, KV_HEADS) == KV_HEADS - 1))
+            def _():
+                leave(path, step, None)
+
+    barrier = pltpu.get_barrier_semaphore()
+    for target in ((up, me), (down, me), (place, before)):
+        pl.semaphore_signal(barrier, inc=1, device_id=target, device_id_type=MESH)
+    own_copy(0, 0).start()
+    query_copy(0).start()
+    for copy in infos:
+        copy.start()
+    own_copy(1, 0).start()
+    own_copy(0, 0).wait()
+    query_copy(0).wait()
     for copy in infos:
         copy.wait()
+    own_copy(1, 0).wait()
     for path in range(2):
         build_bias(path, TREE_MOST - 1)
-    pl.semaphore_wait(barrier, 4)
+    for members in ((0,), (1,), (2, 3), (4, 5, 6, 7)):
+        for path in range(2):
+            attend(path, 0, members)
+        if members == (0,):
+            pl.semaphore_wait(barrier, 3)
+        for path in range(2):
+            leave(path, 0, members)
+        if members == (0,):
+            for head in range(1, KV_HEADS):
+                own_copy(0, head).start()
+                own_copy(1, head).start()
+            for step in range(1, AHEAD + 1):
+                query_copy(step).start()
     for copy in halo:
         copy.start()
-    own_copy(0, 0).wait()
-    own_copy(1, 0).wait()
-    fetch(0)
-    for members in ((0,), (1,), (2, 3), (4, 5, 6, 7)):
-        for path in range(2):
-            attend(path, 0, members)
-        for path in range(2):
-            leave(path, 0, members)
     for head in range(1, KV_HEADS):
         own_copy(0, head).wait()
         own_copy(1, head).wait()
@@ -236,21 +246,42 @@
             build_bias(path, block)
     pl.loop(half, STEPS)(work)
 
-    @pl.loop(0, STEPS)
+    def settle(step, members):
+        for path in range(2):
+
+            @pl.when(place != edges[path])
+            def _():
+                away(path, step, members).wait_send()
+
+            @pl.when(place != edges[1 - path])
+            def _():
+                away(path, step, members).wait_recv()
+
+            @pl.when(place == edges[path])
+            def _():
+                stay(path, step, members).wait()
+
+    @pl.loop(0, KV_HEADS)
     def _(step):
-        for path in range(2):
-
-            @pl.when(place != edges[path])
-            def _():
-                away(path, step, every).wait_send()
-
-            @pl.when(place != edges[1 - path])
-            def _():
-                away(path, step, every).wait_recv()
-
-            @pl.when(place == edges[path])
-            def _():
-                stay(path, step, every).wait()
+        settle(step, every)
+
+    @pl.loop(1, BLOCKS)
+    def _(block):
+        settle(block * KV_HEADS + KV_HEADS - 1, None)
+
+
+def flush(forward, returned, forward_out, returned_out, sem):
+    copies = []
+    for source, target in ((forward, forward_out), (returned, returned_out)):
+        for index in range(PIECES):
+            rows = pl.ds(index * (ROWS // PIECES), ROWS // PIECES)
+            copies.append(
+                pltpu.make_async_copy(source.at[rows], target.at[rows], sem.at[len(copies)])
+            )
+    for copy in copies:
+        copy.start()
+    for copy in copies:
+        copy.wait()
 
 
 def on_device(queries, keys, values, segment, parent, tree_lengths):
@@ -284,6 +315,16 @@
         ),
         name="relay",
     )(*[pltpu.with_memory_space_constraint(x[0], pltpu.HBM) for x in (queries, keys, values, segment, parent)])
+    anywhere = [pl.BlockSpec(memory_space=pl.ANY)] * 2
+    forward, returned = pl.pallas_call(
+        flush,
+        out_shape=(out, out),
+        in_specs=anywhere,
+        out_specs=anywhere,
+        scratch_shapes=[pltpu.SemaphoreType.DMA((2 * PIECES,))],
+        compiler_params=pltpu.CompilerParams(vmem_limit_bytes=1 << 20),
+        name="flush",
+    )(forward, returned)
     return (forward[None], returned[None])
 
 

time: 102 us -> 100 us (0.980)
  local copies, waits for them, and re-layouts: 4.03 us -> 0 us
  Pallas kernels: 97.1 us -> 99.1 us
    unnamed x2 -> x0, local copies, waits for them, and re-layouts: 4.03 us -> none
    pallas_call x0 -> x1, Pallas kernels: none -> 3.37 us  [on_device(): pl.pallas_call(flush, out_shape=(out, out), in_specs=anywhere, out_specs=...]
    pallas_call x1, Pallas kernels: 97.1 us -> 95.7 us  [on_device(): pl.pallas_call(kernel, out_shape=(out, out), in_specs=[pl.BlockSpec(memor...]
where the time goes in v3:
time: 100 us; the launch traced here: 99.7 us
  Pallas kernels  99.1 us (99%)
    pallas_call x1, Pallas kernels, on_device(): pl.pallas_call(kernel, out_shape=(out, out), in_specs=[pl.BlockSpec(memor...  95.7 us
    pallas_call x1, Pallas kernels, on_device(): pl.pallas_call(flush, out_shape=(out, out), in_specs=anywhere, out_specs=...  3.37 us

profile of v3, /device:TPU:0, one launch (start us, length us, event | category | flops | bytes accessed | tf_op | source)
XLA Modules:
  0.0 99.7 jit_solution(4318491177780527443)
XLA Ops:
  0.6 95.7 %relay.1 = (bf16[512,4096]{1,0:T(8,128)(2,1)S(1)}, bf16[512,4096]{1,0:T(8,128)(2,1)S(1)}) custom-call(bf16[2,512,4096]{2,1,0:T(8,128)(2,1)} %bitcast.7, bf16[2,512,512]{2,1,0:T(8,128)(2,1)} %bitcast.8, bf16[2,512,512]{2,1,0:T(8,128)(2,1)} %bitcast.9, s32[2,512]{1,0:T(2,128)} %bitcast.10, s32[2,512]{1,0:T(2,128)} %bitcast.11), custom_call_target="tpu_custom_call" | custom-call | tf_op jit(solution)/shard_map/relay/pallas_call | solution.py:291
  96.3 3.4 %flush.1 = (bf16[512,4096]{1,0:T(8,128)(2,1)}, bf16[512,4096]{1,0:T(8,128)(2,1)}) custom-call(bf16[512,4096]{1,0:T(8,128)(2,1)S(1)} %get-tuple-element.6.forward, bf16[512,4096]{1,0:T(8,128)(2,1)S(1)} %get-tuple-element.7.returned), custom_call_target="tpu_custom_call" | custom-call | tf_op jit(solution)/shard_map/flush/pallas_call | solution.py:319

commit v4 on v3

--- a/solution.py
+++ b/solution.py
@@ -30,7 +30,7 @@
     queries, keys, values, segment, parent,
     forward, returned,
     qbuf, kbuf, vbuf, segbuf, parbuf, bias, stage,
-    qsem, infosem, ownsem, halo_send, halo_recv, send, land_forward, land_returned,
+    qsem, headsem, infosem, ownsem, halo_send, halo_recv, send, land_forward, land_returned,
 ):
     n_pipe, n_dp = lax.axis_size("pipe"), lax.axis_size("dp")
     place, me = lax.axis_index("pipe"), lax.axis_index("dp")
@@ -203,19 +203,27 @@
     barrier = pltpu.get_barrier_semaphore()
     for target in ((up, me), (down, me), (place, before)):
         pl.semaphore_signal(barrier, inc=1, device_id=target, device_id_type=MESH)
-    own_copy(0, 0).start()
-    query_copy(0).start()
+    opening_rows = pl.ds((TREE_MOST - 1) * BLK, BLK)
+    heads = [
+        pltpu.make_async_copy(
+            queries.at[:, opening_rows, lanes], qbuf.at[:, opening_rows, lanes], headsem.at[index]
+        )
+        for index, lanes in enumerate((pl.ds(0, HEAD), pl.ds(HEAD, WIDE - HEAD)))
+    ]
     for copy in infos:
         copy.start()
+    own_copy(0, 0).start()
+    heads[0].start()
     own_copy(1, 0).start()
+    heads[1].start()
     own_copy(0, 0).wait()
-    query_copy(0).wait()
+    heads[0].wait()
     for copy in infos:
         copy.wait()
     own_copy(1, 0).wait()
     for path in range(2):
         build_bias(path, TREE_MOST - 1)
-    for members in ((0,), (1,), (2, 3), (4, 5, 6, 7)):
+    for members in ((0,), (1,), (2,), (3, 4), (5, 6, 7)):
         for path in range(2):
             attend(path, 0, members)
         if members == (0,):
@@ -228,6 +236,7 @@
                 own_copy(1, head).start()
             for step in range(1, AHEAD + 1):
                 query_copy(step).start()
+            heads[1].wait()
     for copy in halo:
         copy.start()
     for head in range(1, KV_HEADS):
@@ -302,6 +311,7 @@
             pltpu.VMEM((2 * BLOCKS, BLK, SPAN), jnp.float32),
             pltpu.VMEM((2, ROWS, width), jnp.bfloat16),
             pltpu.SemaphoreType.DMA((STEPS,)),
+            pltpu.SemaphoreType.DMA((2,)),
             pltpu.SemaphoreType.DMA((2,)),
             pltpu.SemaphoreType.DMA((2, KV_HEADS)),
             pltpu.SemaphoreType.DMA((4,)),

time: 100 us -> 100 us (level)
  no operation moved by 1% of the time
where the time goes in v4:
time: 100 us; the launch traced here: 99.6 us
  Pallas kernels  98.9 us (99%)
    pallas_call x1, Pallas kernels, on_device(): pl.pallas_call(kernel, out_shape=(out, out), in_specs=[pl.BlockSpec(memor...  95.6 us
    pallas_call x1, Pallas kernels, on_device(): pl.pallas_call(flush, out_shape=(out, out), in_specs=anywhere, out_specs=...  3.37 us

profile of v4, /device:TPU:0, one launch (start us, length us, event | category | flops | bytes accessed | tf_op | source)
XLA Modules:
  0.0 99.6 jit_solution(3436003557471027346)
XLA Ops:
  0.6 95.6 %relay.1 = (bf16[512,4096]{1,0:T(8,128)(2,1)S(1)}, bf16[512,4096]{1,0:T(8,128)(2,1)S(1)}) custom-call(bf16[2,512,4096]{2,1,0:T(8,128)(2,1)} %bitcast.7, bf16[2,512,512]{2,1,0:T(8,128)(2,1)} %bitcast.8, bf16[2,512,512]{2,1,0:T(8,128)(2,1)} %bitcast.9, s32[2,512]{1,0:T(2,128)} %bitcast.10, s32[2,512]{1,0:T(2,128)} %bitcast.11), custom_call_target="tpu_custom_call" | custom-call | tf_op jit(solution)/shard_map/relay/pallas_call | solution.py:300
  96.2 3.4 %flush.1 = (bf16[512,4096]{1,0:T(8,128)(2,1)}, bf16[512,4096]{1,0:T(8,128)(2,1)}) custom-call(bf16[512,4096]{1,0:T(8,128)(2,1)S(1)} %get-tuple-element.6.forward, bf16[512,4096]{1,0:T(8,128)(2,1)S(1)} %get-tuple-element.7.returned), custom_call_target="tpu_custom_call" | custom-call | tf_op jit(solution)/shard_map/flush/pallas_call | solution.py:329

commit v5 on v3

--- a/solution.py
+++ b/solution.py
@@ -201,8 +201,13 @@
                 leave(path, step, None)
 
     barrier = pltpu.get_barrier_semaphore()
-    for target in ((up, me), (down, me), (place, before)):
-        pl.semaphore_signal(barrier, inc=1, device_id=target, device_id_type=MESH)
+    for target, met in (((up, me), place < n_pipe - 1), ((down, me), place > 0)):
+
+        @pl.when(met)
+        def _():
+            pl.semaphore_signal(barrier, inc=1, device_id=target, device_id_type=MESH)
+
+    pl.semaphore_signal(barrier, inc=1, device_id=(place, before), device_id_type=MESH)
     own_copy(0, 0).start()
     query_copy(0).start()
     for copy in infos:
@@ -219,7 +224,7 @@
         for path in range(2):
             attend(path, 0, members)
         if members == (0,):
-            pl.semaphore_wait(barrier, 3)
+            pl.semaphore_wait(barrier, jnp.where((place > 0) & (place < n_pipe - 1), 3, 2))
         for path in range(2):
             leave(path, 0, members)
         if members == (0,):

time: 100 us -> 100 us (level)
  no operation moved by 1% of the time
where the time goes in v5:
time: 100 us; the launch traced here: 99.7 us
  Pallas kernels  99.1 us (99%)
    pallas_call x1, Pallas kernels, on_device(): pl.pallas_call(kernel, out_shape=(out, out), in_specs=[pl.BlockSpec(memor...  95.7 us
    pallas_call x1, Pallas kernels, on_device(): pl.pallas_call(flush, out_shape=(out, out), in_specs=anywhere, out_specs=...  3.37 us

profile of v5, /device:TPU:0, one launch (start us, length us, event | category | flops | bytes accessed | tf_op | source)
XLA Modules:
  0.0 99.7 jit_solution(9120567453225229551)
XLA Ops:
  0.6 95.7 %relay.1 = (bf16[512,4096]{1,0:T(8,128)(2,1)S(1)}, bf16[512,4096]{1,0:T(8,128)(2,1)S(1)}) custom-call(bf16[2,512,4096]{2,1,0:T(8,128)(2,1)} %bitcast.7, bf16[2,512,512]{2,1,0:T(8,128)(2,1)} %bitcast.8, bf16[2,512,512]{2,1,0:T(8,128)(2,1)} %bitcast.9, s32[2,512]{1,0:T(2,128)} %bitcast.10, s32[2,512]{1,0:T(2,128)} %bitcast.11), custom_call_target="tpu_custom_call" | custom-call | tf_op jit(solution)/shard_map/relay/pallas_call | solution.py:296
  96.3 3.4 %flush.1 = (bf16[512,4096]{1,0:T(8,128)(2,1)}, bf16[512,4096]{1,0:T(8,128)(2,1)}) custom-call(bf16[512,4096]{1,0:T(8,128)(2,1)S(1)} %get-tuple-element.6.forward, bf16[512,4096]{1,0:T(8,128)(2,1)S(1)} %get-tuple-element.7.returned), custom_call_target="tpu_custom_call" | custom-call | tf_op jit(solution)/shard_map/flush/pallas_call | solution.py:324
